TPU v7x, 256 devices: a whole 4x4x8 slice. The times are simulated.
256 devices in a mesh: mic: 4 (over y), seq: 64 (over z, x, core).
Axes of the slice: x: 4, y: 4, z: 8, core: 2. Of those that a mesh axis runs over, the one named last changes fastest.
Arguments:
- frames_in: bfloat16 [8, 32768, 512], P('mic', 'seq'), may hold values from -16 to 16
- w_qkv: bfloat16 [8, 512, 1536], P('mic'), may hold values from -0.25 to 0.25
- w_join: bfloat16 [4096, 1024], P(('mic', 'seq')), may hold values from -0.09375 to 0.09375
- norm_gain: float32 [1024], replicated, may hold values from 0.5 to 2
- w_router: bfloat16 [1024, 64], replicated, may hold values from -0.1875 to 0.1875
- w_gate: bfloat16 [64, 1024, 4096], P('seq', None, 'mic'), may hold values from -0.1875 to 0.1875
- w_up: bfloat16 [64, 1024, 4096], P('seq', None, 'mic'), may hold values from -0.1875 to 0.1875
- w_down: bfloat16 [64, 4096, 1024], P('seq', 'mic'), may hold values from -0.09375 to 0.09375
- expert_ids: int32 [64, 4, 128, 2], P('seq', 'mic'), may hold values from 0 to 63, all different within a row; in each aligned block of 128 rows (0 to 127, 128 to 255, ..., all dimensions but the last counted through in order) at most 6 rows name the same one
Outputs:
- layer_out: bfloat16 [64, 4, 128, 1024], P('seq', 'mic')
Inputs may be any that keep to these rules, and one draw needn't show every extreme that they name: `expert_ids`: in the rows of one block (128 frames) no expert is named more than 6 times, a bound that some block reaches; the two ids of a frame differ.
All inputs are finite; a program needn't handle non-finite values.
Results may differ from a plain program's by a relative error of at most 0.017.
Values may be sent and summed in bfloat16 or wider, within the bound.
A program may use at most 128 MiB of HBM per device.

v0:
```python
import jax
import jax.numpy as jnp
from jax import lax
from jax.sharding import PartitionSpec as P

MICS = 8
HEADS = 8
TOP = 2


def body(frames_in, w_qkv, w_join, norm_gain, w_router, w_gate, w_up, w_down, expert_ids):
    mic_count = lax.axis_size("mic")
    seq_count = lax.axis_size("seq")
    mic_local, span, chan_width = frames_in.shape
    frame_rows = span // mic_count
    head_dim = chan_width // HEADS
    model_width = w_join.shape[1]
    expert_count = w_router.shape[1]
    exp_local = w_gate.shape[0]
    capacity = max(2, 3 * TOP * frame_rows // (2 * expert_count))
    projected = jnp.einsum(
        "mfc,mce->mfe", frames_in, w_qkv, preferred_element_type=jnp.float32
    ).astype(jnp.bfloat16)
    projected = projected.reshape(mic_local, mic_count, frame_rows, 3 * chan_width)
    arrived_block = lax.all_to_all(projected, "mic", split_axis=1, concat_axis=0, tiled=True)
    arrived_block = arrived_block[:, 0]
    frame_count = arrived_block.shape[1]
    queries = arrived_block[..., :chan_width].reshape(MICS, frame_count, HEADS, head_dim)
    keys_all = arrived_block[..., chan_width : 2 * chan_width].reshape(
        MICS, frame_count, HEADS, head_dim
    )
    values_all = arrived_block[..., 2 * chan_width :].reshape(MICS, frame_count, HEADS, head_dim)
    scores = jnp.einsum(
        "ifhd,jfhd->fhij", queries, keys_all, preferred_element_type=jnp.float32
    ) * head_dim ** (-0.5)
    row_max = jnp.max(scores, axis=-1, keepdims=True)
    weights = jnp.exp(scores - row_max)
    probs = (weights / jnp.sum(weights, axis=-1, keepdims=True)).astype(jnp.bfloat16)
    mixed_heads = jnp.einsum(
        "fhij,jfhd->fihd", probs, values_all, preferred_element_type=jnp.float32
    )
    attended = mixed_heads.astype(jnp.bfloat16).reshape(frame_count, MICS * chan_width)
    joined = jnp.dot(
        attended,
        lax.all_gather(w_join, ("mic", "seq"), axis=0, tiled=True),
        preferred_element_type=jnp.float32,
    )
    scale_row = lax.rsqrt(jnp.mean(joined * joined, axis=-1, keepdims=True) + 1e-06)
    normed = (joined * scale_row * norm_gain).astype(jnp.bfloat16)
    logits = jnp.dot(normed, w_router, preferred_element_type=jnp.float32)
    expert_rows = expert_ids.reshape(frame_rows, TOP)
    chosen = (expert_rows[..., None] == jnp.arange(expert_count, dtype=jnp.int32)).astype(jnp.int32)
    picked = jnp.sum(logits[:, None, :] * chosen.astype(jnp.float32), axis=-1)
    first_gate = 1.0 / (1.0 + jnp.exp(picked[:, 1] - picked[:, 0]))
    gates = jnp.stack([first_gate, 1.0 - first_gate], axis=-1)
    counts = jnp.sum(chosen, axis=1)
    before = jnp.cumsum(counts, axis=0) - counts
    slot_index = jnp.sum(before[:, None, :] * chosen, axis=-1)
    in_slot = slot_index[..., None] == jnp.arange(capacity, dtype=jnp.int32)
    mapped = (
        ((chosen[..., :, None] == 1) & in_slot[..., None, :])
        .reshape(frame_rows, TOP, expert_count * capacity)
        .astype(jnp.bfloat16)
    )
    merged_map = jnp.sum(mapped, axis=1)
    buffers = jnp.einsum(
        "rs,rd->sd", merged_map, normed, preferred_element_type=jnp.float32
    ).astype(jnp.bfloat16)
    buffers = buffers.reshape(seq_count, exp_local * capacity, model_width)
    landed = lax.all_to_all(buffers, "seq", split_axis=0, concat_axis=0, tiled=True)
    arrived = lax.all_gather(landed[None], "mic", axis=0, tiled=True)
    flat = arrived.reshape(mic_count * seq_count * exp_local * capacity, model_width)
    piece_rows = flat.reshape(-1, exp_local, capacity, model_width)
    first_proj = jnp.einsum(
        "nejd,edf->nejf", piece_rows, w_gate, preferred_element_type=jnp.float32
    )
    second_proj = jnp.einsum("nejd,edf->nejf", piece_rows, w_up, preferred_element_type=jnp.float32)
    inner = (jax.nn.silu(first_proj) * second_proj).astype(jnp.bfloat16)
    result = jnp.einsum("nejf,efd->nejd", inner, w_down, preferred_element_type=jnp.float32)
    summed = lax.psum_scatter(
        result.reshape(
            lax.axis_size("mic") * (seq_count * exp_local * capacity), model_width
        ).astype(jnp.bfloat16),
        "mic",
        scatter_dimension=0,
        tiled=True,
    ).astype(jnp.float32)
    summed = summed.astype(jnp.bfloat16).reshape(seq_count, exp_local * capacity, model_width)
    returned = lax.all_to_all(summed, "seq", split_axis=0, concat_axis=0, tiled=True)
    returned = returned.reshape(expert_count * capacity, model_width)
    picked_out = jnp.einsum("rks,sd->rkd", mapped, returned, preferred_element_type=jnp.float32)
    total = joined + jnp.sum(gates[..., None] * picked_out, axis=1)
    return total.astype(jnp.bfloat16).reshape(1, 1, frame_rows, model_width)


def solution(mesh):
    return jax.shard_map(
        body,
        mesh=mesh,
        in_specs=(
            P("mic", "seq", None),
            P("mic", None, None),
            P(("mic", "seq"), None),
            P(),
            P(),
            P("seq", None, "mic"),
            P("seq", None, "mic"),
            P("seq", "mic", None),
            P("seq", "mic", None, None),
        ),
        out_specs=P("seq", "mic", None, None),
        check_vma=False,
    )
```

profile of v0, /device:TPU:1, one launch (start us, length us, event | category | flops | bytes accessed | tf_op | source)
XLA Modules:
  0.0 346.4 jit_solution(7928431488291336185)
XLA Ops:
  6.5 0.0 copy-start
  6.5 0.0 all-gather.4.cloned.1.call-start
  6.5 0.7 all-gather.4.cloned.1.call-update
  7.3 1.2 copy-done
  8.4 3.0 convolution_convert_fusion
  11.5 2.0 copy.26
  13.4 5.1 %all-to-all-start = ((bf16[2,4,128,1536]{3,2,0,1:T(8,128)(2,1)}), bf16[2,4,128,1536]{3,2,0,1:T(8,128)(2,1)S(1)}, u32[]{:S(2)}, u32[]{:S(2)}) async-start(bf16[2,4,128,1536]{3,2,0,1:T(8,128)(2,1)} %copy.26), calls=%async_computation | async-start | bytes 6291456 | tf_op jit(solution)/shard_map/all_to_all | solution.py:25
  18.6 0.0 all-gather.6.cloned.1.call-start
  18.6 0.0 copy-done.8
  18.6 0.1 copy.35
  18.7 0.2 reduce_window_sum.11
  18.9 0.1 copy.37
  19.1 0.1 copy.38
  19.2 35.4 %all-to-all-done = bf16[2,4,128,1536]{3,2,0,1:T(8,128)(2,1)S(1)} async-done(((bf16[2,4,128,1536]{3,2,0,1:T(8,128)(2,1)}), bf16[2,4,128,1536]{3,2,0,1:T(8,128)(2,1)S(1)}, u32[]{:S(2)}, u32[]{:S(2)}) %all-to-all-start) | async-done | bytes 3145760 | tf_op jit(solution)/shard_map/all_to_all | solution.py:25
  54.6 1.7 fusion.37
  56.4 1.7 copy.28
  58.1 3.8 %copy.30 = bf16[8,128,8,64]{3,0,2,1:T(8,128)(2,1)} copy(bf16[8,128,8,64]{1,3,2,0:T(8,128)(2,1)S(1)} %bitcast.103) | data formatting | bytes 2097152 | tf_op jit(solution)/shard_map/reshape | solution.py:28
  61.8 0.0 copy-done.4
  61.8 0.7 copy.29
  62.5 3.7 %copy.31 = bf16[8,128,8,64]{3,0,2,1:T(8,128)(2,1)} copy(bf16[8,128,8,64]{1,3,2,0:T(8,128)(2,1)S(1)} %bitcast.104) | data formatting | bytes 2097152 | tf_op jit(solution)/shard_map/reshape | solution.py:29
  66.2 0.0 copy-done.3
  66.2 0.7 copy.27
  66.9 3.7 %copy.32 = bf16[8,128,8,64]{3,0,2,1:T(8,128)(2,1)} copy(bf16[8,128,8,64]{1,3,2,0:T(8,128)(2,1)S(1)} %bitcast.105) | data formatting | bytes 2097152 | tf_op jit(solution)/shard_map/reshape | solution.py:32
  70.6 0.0 copy-done.5
  70.6 6.6 %fusion.38 = (f32[128,8,8]{2,1,0:T(8,128)S(1)}, f32[128,8,8,8]{2,3,1,0:T(8,128)}) fusion(bf16[8,128,8,64]{3,0,2,1:T(8,128)(2,1)S(1)} %copy-done.5, bf16[8,128,8,64]{3,0,2,1:T(8,128)(2,1)} %copy.31), kind=kOutput, calls=%fused_computation.56 | convolution fusion | flops 8585223 | bytes 2392064 | tf_op jit(solution)/shard_map/sub | solution.py:37
  77.2 4.7 %convert_bitcast_fusion.1 = bf16[128,8,8,64]{3,1,2,0:T(8,128)(2,1)} fusion(bf16[8,128,8,64]{3,0,2,1:T(8,128)(2,1)} %copy.32, f32[128,8,8,8]{2,3,1,0:T(8,128)} %get-tuple-element.11, f32[128,8,8]{2,1,0:T(8,128)S(1)} %get-tuple-element.10), kind=kOutput, calls=%fused_computation.22 | convolution fusion | flops 9043968 | bytes 2392064 | tf_op jit(solution)/shard_map/fhij,jfhd->fihd/dot_general | solution.py:39
  81.9 3.2 copy.34
  85.1 59.5 %all-gather.4.cloned.1.call-done = bf16[4096,1024]{1,0:T(8,128)(2,1)} async-done(((bf16[16,1024]{1,0:T(8,128)(2,1)}), bf16[4096,1024]{1,0:T(8,128)(2,1)}) %all-gather.4.cloned.1.call-update) | async-done | bytes 8388624 | tf_op jit(solution)/shard_map/all_gather | solution.py:45
  144.6 4.7 %multiply_reduce_fusion.1 = (f32[128]{0:T(128)S(1)}, f32[128,1024]{1,0:T(8,128)S(1)}) fusion(bf16[128,4096]{0,1:T(8,128)(2,1)S(1)} %bitcast.102, bf16[4096,1024]{1,0:T(8,128)(2,1)} %all-gather.4.cloned.1.call-done), kind=kOutput, calls=%fused_computation.33 | convolution fusion | flops 1074003840 | bytes 9961984 | tf_op jit(solution)/shard_map/dot_general | solution.py:43
  149.3 0.4 convolution_convert_fusion.1
  149.8 0.3 reshape.92
  150.0 35.1 %all_to_all.25 = bf16[64,6,1024]{2,1,0:T(8,128)(2,1)S(1)} all-to-all(bf16[64,6,1024]{2,1,0:T(8,128)(2,1)S(1)} %reshape.92), channel_id=1, replica_groups=mesh['mic'=4,'seq'=64] {'seq'}, dimensions={0} | all-to-all | bytes 1572864 | tf_op jit(solution)/shard_map/all_to_all | solution.py:70
  185.1 1.3 copy.39
  186.4 0.0 all-gather.6.cloned.1.call-update
  186.5 0.0 reduce-scatter.2.cloned.1.call-start
  186.5 37.7 %all-gather.6.cloned.1.call-done = bf16[256,6,1024]{2,0,1:T(8,128)(2,1)} async-done(((bf16[64,6,1024]{2,0,1:T(8,128)(2,1)}), bf16[256,6,1024]{2,0,1:T(8,128)(2,1)}) %all-gather.6.cloned.1.call-update) | async-done | bytes 3145744 | tf_op jit(solution)/shard_map/all_gather | solution.py:71
  224.2 8.6 %fusion.19 = f32[256,6,1024]{2,0,1:T(8,128)} fusion(bf16[256,6,1024]{2,0,1:T(8,128)(2,1)} %all-gather.6.cloned.1.call-done, bf16[1,1024,1024]{2,1,0:T(8,128)(2,1)} %param.14), kind=kOutput, calls=%fused_computation.20 | convolution fusion | flops 3221225472 | bytes 11534336 | tf_op jit(solution)/shard_map/nejd,edf->nejf/dot_general | solution.py:74
  232.8 10.6 %convert_bitcast_fusion = bf16[256,1,6,1024]{3,0,2,1:T(8,128)(2,1)S(1)} fusion(f32[256,6,1024]{2,0,1:T(8,128)} %fusion.19, bf16[256,6,1024]{2,0,1:T(8,128)(2,1)} %all-gather.6.cloned.1.call-done, bf16[1,1024,1024]{2,1,0:T(8,128)(2,1)} %param.16, bf16[1,1024,1024]{2,1,0:T(8,128)(2,1)} %param.15), kind=kOutput, calls=%fused_computation.15 | convolution fusion | flops 6453460992 | bytes 16777216 | tf_op jit(solution)/shard_map/nejf,efd->nejd/dot_general | solution.py:79
  243.4 3.7 %copy.40 = bf16[256,1,6,1024]{3,2,0,1:T(8,128)(2,1)} copy(bf16[256,1,6,1024]{3,0,2,1:T(8,128)(2,1)S(1)} %convert_bitcast_fusion) | data formatting | bytes 6291456 | tf_op jit(solution)/shard_map/convert_element_type | solution.py:83
  247.1 6.3 %convert_element_type.71 = bf16[1536,1024]{1,0:T(8,128)(2,1)} reshape(bf16[256,1,6,1024]{3,2,0,1:T(8,128)(2,1)} %copy.40) | data formatting | bytes 6291456 | tf_op jit(solution)/shard_map/convert_element_type | solution.py:83
  253.4 0.0 reduce-scatter.2.cloned.1.call-update
  253.5 41.3 %reduce-scatter.2.cloned.1.call-done = bf16[384,1024]{1,0:T(8,128)(2,1)} async-done(((bf16[1536,1024]{1,0:T(8,128)(2,1)}), bf16[384,1024]{1,0:T(8,128)(2,1)}) %reduce-scatter.2.cloned.1.call-update) | async-done | bytes 786448 | tf_op jit(solution)/shard_map/reduce_scatter | solution.py:80
  294.7 2.3 reshape.98
  297.1 10.8 %all-to-all-start.2 = ((bf16[64,6,1024]{2,1,0:T(8,128)(2,1)}), bf16[64,6,1024]{2,1,0:T(8,128)(2,1)}, u32[]{:S(2)}, u32[]{:S(2)}) async-start(bf16[64,6,1024]{2,1,0:T(8,128)(2,1)} %reshape.98), calls=%async_computation.3 | async-start | bytes 2097152 | tf_op jit(solution)/shard_map/all_to_all | solution.py:89
  307.9 1.3 fusion.36
  309.3 26.5 %all-to-all-done.2 = bf16[64,6,1024]{2,1,0:T(8,128)(2,1)} async-done(((bf16[64,6,1024]{2,1,0:T(8,128)(2,1)}), bf16[64,6,1024]{2,1,0:T(8,128)(2,1)}, u32[]{:S(2)}, u32[]{:S(2)}) %all-to-all-start.2) | async-done | bytes 786464 | tf_op jit(solution)/shard_map/all_to_all | solution.py:89
  335.8 2.3 fusion.24
  338.1 1.8 fusion.28
  (23 shorter events, 0.3 us)
Async XLA Ops:
  6.5 1.9 copy-start
  6.5 138.0 %all-gather.4.cloned.1.call-start = ((), (), s32[]{:S(2)}) async-start(), calls=%async_computation.4 | async-start | bytes 8421376 | tf_op jit(solution)/shard_map/all_gather | solution.py:45
  13.4 5.2 %copy-start.8 = (s32[1,1,128,2]{2,3,1,0:T(2,128)S(1)}, s32[1,1,128,2]{2,3,1,0:T(2,128)}, u32[]{:S(2)}) copy-start(s32[1,1,128,2]{2,3,1,0:T(2,128)} %param.17) | copy-start | bytes 3076
  13.4 41.2 %all-to-all-start = ((bf16[2,4,128,1536]{3,2,0,1:T(8,128)(2,1)}), bf16[2,4,128,1536]{3,2,0,1:T(8,128)(2,1)S(1)}, u32[]{:S(2)}, u32[]{:S(2)}) async-start(bf16[2,4,128,1536]{3,2,0,1:T(8,128)(2,1)} %copy.26), calls=%async_computation | async-start | bytes 6291456 | tf_op jit(solution)/shard_map/all_to_all | solution.py:25
  18.6 205.6 %all-gather.6.cloned.1.call-start = ((), (), s32[]{:S(2)}) async-start(), calls=%async_computation.6 | async-start | bytes 3932160 | tf_op jit(solution)/shard_map/all_gather | solution.py:71
  56.4 5.5 %copy-start.4 = (bf16[8,128,512]{2,1,0:T(8,128)(2,1)S(1)}, bf16[8,128,512]{2,1,0:T(8,128)(2,1)}, u32[]{:S(2)}) copy-start(bf16[8,128,512]{2,1,0:T(8,128)(2,1)} %get-tuple-element.7) | copy-start | bytes 3145732
  61.8 4.4 %copy-start.3 = (bf16[8,128,512]{2,1,0:T(8,128)(2,1)S(1)}, bf16[8,128,512]{2,1,0:T(8,128)(2,1)}, u32[]{:S(2)}) copy-start(bf16[8,128,512]{2,1,0:T(8,128)(2,1)} %get-tuple-element.9) | copy-start | bytes 3145732
  66.9 3.8 %copy-start.5 = (bf16[8,128,8,64]{3,0,2,1:T(8,128)(2,1)S(1)}, bf16[8,128,8,64]{3,0,2,1:T(8,128)(2,1)}, u32[]{:S(2)}) copy-start(bf16[8,128,8,64]{3,0,2,1:T(8,128)(2,1)} %copy.30) | copy-start | bytes 3145732
  144.6 4.8 %copy-start.7 = (f32[1024]{0:T(1024)S(1)}, f32[1024]{0:T(1024)}, u32[]{:S(2)}) copy-start(f32[1024]{0:T(1024)} %param.12) | copy-start | bytes 12292
  149.3 37.1 %copy-start.2 = (f32[128,1024]{1,0:T(8,128)}, f32[128,1024]{1,0:T(8,128)S(1)}, u32[]{:S(2)}) copy-start(f32[128,1024]{1,0:T(8,128)S(1)} %get-tuple-element.13) | copy-start | bytes 1572868
  186.5 108.3 %reduce-scatter.2.cloned.1.call-start = ((), (), s32[]{:S(2)}) async-start(), calls=%async_computation.5 | async-start | bytes 3932160 | tf_op jit(solution)/shard_map/reduce_scatter | solution.py:80
  253.4 54.4 %copy-start.6 = (bf16[1024,64]{0,1:T(8,128)(2,1)S(1)}, bf16[1024,64]{0,1:T(8,128)(2,1)}, u32[]{:S(2)}) copy-start(bf16[1024,64]{0,1:T(8,128)(2,1)} %param.13) | copy-start | bytes 393220
  294.7 45.2 %copy-start.1 = (bf16[2,512,1536]{2,1,0:T(8,128)(2,1)S(1)}, bf16[2,512,1536]{2,1,0:T(8,128)(2,1)}, u32[]{:S(2)}) copy-start(bf16[2,512,1536]{2,1,0:T(8,128)(2,1)} %param.10) | copy-start | bytes 9437188
  297.1 38.7 %all-to-all-start.2 = ((bf16[64,6,1024]{2,1,0:T(8,128)(2,1)}), bf16[64,6,1024]{2,1,0:T(8,128)(2,1)}, u32[]{:S(2)}, u32[]{:S(2)}) async-start(bf16[64,6,1024]{2,1,0:T(8,128)(2,1)} %reshape.98), calls=%async_computation.3 | async-start | bytes 2097152 | tf_op jit(solution)/shard_map/all_to_all | solution.py:89
Sparse Core Ops, SparseCore 0:
  10.9 133.5 all-gather.3
  186.6 37.5 all-gather.5
  253.6 41.0 reduce-scatter.1
where the time goes:
time: 347 us; the launch traced here: 346 us
  waiting for transfers between devices  201 us (58%)
  matrix products  42.3 us (12%)
  local copies, waits for them, and re-layouts  36.6 us (11%)
  blocking collectives  35.1 us (10%)
  starting transfers between devices  16 us (5%)
  between operations  13.3 us (4%)
    all_gather x1, waiting for transfers between devices, body(): lax.all_gather(w_join, ('mic', 'seq'), axis=0, tiled=True)  59.5 us
    reduce_scatter x1, waiting for transfers between devices, body(): lax.psum_scatter(result.reshape(lax.axis_size('mic') * (seq_count * exp_l...  41.3 us
    all_gather x1, waiting for transfers between devices, body(): arrived = lax.all_gather(landed[None], 'mic', axis=0, tiled=True)  37.7 us
    all_to_all x1, waiting for transfers between devices, body(): lax.all_to_all(projected, 'mic', split_axis=1, concat_axis=0, tiled=True)  35.4 us
    all_to_all x1, blocking collectives, body(): lax.all_to_all(buffers, 'seq', split_axis=0, concat_axis=0, tiled=True)  35.1 us
    all_to_all x1, waiting for transfers between devices, body(): lax.all_to_all(summed, 'seq', split_axis=0, concat_axis=0, tiled=True)  26.5 us
    all_to_all x1, starting transfers between devices, body(): lax.all_to_all(summed, 'seq', split_axis=0, concat_axis=0, tiled=True)  10.8 us
    dot_general x1, matrix products, body(): jnp.einsum('nejf,efd->nejd', inner, w_down, preferred_element_type=jnp.fl...  10.6 us
  transfers between devices with their start and end apart: 5, of which 5 were waited for; matrix products, arithmetic and copies ran while one was open for 11% of the time, Pallas kernels for 0%

commit v1 on v0

v1 whole, which is shorter than its diff:
```python
import jax
import jax.numpy as jnp
from jax import lax
from jax.experimental import pallas as pl
from jax.experimental.pallas import tpu as pltpu
from jax.sharding import PartitionSpec as P

MICS = 8
HEADS = 8
TOP = 2


def attend_kernel(x_ref, o_ref):
    mics = x_ref.shape[0]
    width = x_ref.shape[1] // 3
    head_dim = width // HEADS
    scale = head_dim ** (-0.5)

    def head(h, carry):
        base = pl.multiple_of(h * head_dim, head_dim)
        keys = [
            x_ref[j, pl.ds(width + base, head_dim), :].astype(jnp.float32)
            for j in range(mics)
        ]
        for i in range(mics):
            q = x_ref[i, pl.ds(base, head_dim), :].astype(jnp.float32)
            s = [jnp.sum(q * keys[j], axis=0, keepdims=True) * scale for j in range(mics)]
            m = s[0]
            for j in range(1, mics):
                m = jnp.maximum(m, s[j])
            e = [jnp.exp(s[j] - m) for j in range(mics)]
            den = e[0]
            for j in range(1, mics):
                den = den + e[j]
            acc = jnp.zeros((head_dim, x_ref.shape[2]), jnp.float32)
            for j in range(mics):
                p = (e[j] / den).astype(jnp.bfloat16).astype(jnp.float32)
                v = x_ref[j, pl.ds(2 * width + base, head_dim), :].astype(jnp.float32)
                acc = acc + p * v
            o_ref[i, pl.ds(base, head_dim), :] = acc.astype(o_ref.dtype)
        return carry

    lax.fori_loop(0, HEADS, head, 0)


def attend(x):
    mics, rows, frames = x.shape
    return pl.pallas_call(
        attend_kernel,
        out_shape=jax.ShapeDtypeStruct((mics, rows // 3, frames), jnp.bfloat16),
        in_specs=[pl.BlockSpec(memory_space=pltpu.VMEM)],
        out_specs=pl.BlockSpec(memory_space=pltpu.VMEM),
        cost_estimate=pl.CostEstimate(
            flops=4 * mics * mics * (rows // 3) * frames,
            transcendentals=mics * mics * HEADS * frames,
            bytes_accessed=x.size * 2 + mics * (rows // 3) * frames * 2,
        ),
    )(x)


def body(frames_in, w_qkv, w_join, norm_gain, w_router, w_gate, w_up, w_down, expert_ids):
    mic_count = lax.axis_size("mic")
    seq_count = lax.axis_size("seq")
    mic_local, span, chan_width = frames_in.shape
    frame_rows = span // mic_count
    model_width = w_join.shape[1]
    expert_count = w_router.shape[1]
    exp_local = w_gate.shape[0]
    capacity = max(2, 3 * TOP * frame_rows // (2 * expert_count))

    projected = jnp.einsum(
        "mfc,mce->mef", frames_in, w_qkv, preferred_element_type=jnp.float32
    ).astype(jnp.bfloat16)
    projected = projected.reshape(mic_local, 3 * chan_width, mic_count, frame_rows)
    arrived = lax.all_to_all(projected, "mic", split_axis=2, concat_axis=0, tiled=True)
    arrived = arrived.reshape(MICS, 3 * chan_width, frame_rows)
    attended_t = attend(arrived).reshape(mic_count, MICS * chan_width // mic_count, frame_rows)

    cols = lax.all_to_all(attended_t, "mic", split_axis=0, concat_axis=2, tiled=True)
    cols = cols.reshape(MICS * chan_width // mic_count, mic_count * frame_rows)
    w_rows = lax.all_gather(w_join, "seq", axis=0, tiled=True)
    partial = lax.dot_general(
        cols, w_rows, (((0,), (0,)), ((), ())), preferred_element_type=jnp.float32
    ).astype(jnp.bfloat16)
    joined = lax.psum_scatter(partial, "mic", scatter_dimension=0, tiled=True).astype(jnp.float32)

    scale_row = lax.rsqrt(jnp.mean(joined * joined, axis=-1, keepdims=True) + 1e-06)
    normed = (joined * scale_row * norm_gain).astype(jnp.bfloat16)
    logits = jnp.dot(normed, w_router, preferred_element_type=jnp.float32)
    expert_rows = expert_ids.reshape(frame_rows, TOP)
    chosen = (expert_rows[..., None] == jnp.arange(expert_count, dtype=jnp.int32)).astype(jnp.int32)
    picked = jnp.sum(logits[:, None, :] * chosen.astype(jnp.float32), axis=-1)
    first_gate = 1.0 / (1.0 + jnp.exp(picked[:, 1] - picked[:, 0]))
    gates = jnp.stack([first_gate, 1.0 - first_gate], axis=-1)
    counts = jnp.sum(chosen, axis=1)
    before = jnp.cumsum(counts, axis=0) - counts
    slot_index = jnp.sum(before[:, None, :] * chosen, axis=-1)
    in_slot = slot_index[..., None] == jnp.arange(capacity, dtype=jnp.int32)
    mapped = (
        ((chosen[..., :, None] == 1) & in_slot[..., None, :])
        .reshape(frame_rows, TOP, expert_count * capacity)
        .astype(jnp.bfloat16)
    )
    merged_map = jnp.sum(mapped, axis=1)
    buffers = jnp.einsum(
        "rs,rd->sd", merged_map, normed, preferred_element_type=jnp.float32
    ).astype(jnp.bfloat16)
    buffers = buffers.reshape(seq_count, exp_local * capacity, model_width)
    landed = lax.all_to_all(buffers, "seq", split_axis=0, concat_axis=0, tiled=True)
    arrived_rows = lax.all_gather(landed[None], "mic", axis=0, tiled=True)
    flat = arrived_rows.reshape(mic_count * seq_count * exp_local * capacity, model_width)
    first_proj = jnp.dot(flat, w_gate[0], preferred_element_type=jnp.float32)
    second_proj = jnp.dot(flat, w_up[0], preferred_element_type=jnp.float32)
    inner = (jax.nn.silu(first_proj) * second_proj).astype(jnp.bfloat16)
    result = jnp.dot(inner, w_down[0], preferred_element_type=jnp.float32).astype(jnp.bfloat16)
    summed = lax.psum_scatter(result, "mic", scatter_dimension=0, tiled=True)
    summed = summed.reshape(seq_count, exp_local * capacity, model_width)
    returned = lax.all_to_all(summed, "seq", split_axis=0, concat_axis=0, tiled=True)
    returned = returned.reshape(expert_count * capacity, model_width)
    picked_out = jnp.einsum("rks,sd->rkd", mapped, returned, preferred_element_type=jnp.float32)
    total = joined + jnp.sum(gates[..., None] * picked_out, axis=1)
    return total.astype(jnp.bfloat16).reshape(1, 1, frame_rows, model_width)


def solution(mesh):
    return jax.shard_map(
        body,
        mesh=mesh,
        in_specs=(
            P("mic", "seq", None),
            P("mic", None, None),
            P(("mic", "seq"), None),
            P(),
            P(),
            P("seq", None, "mic"),
            P("seq", None, "mic"),
            P("seq", "mic", None),
            P("seq", "mic", None, None),
        ),
        out_specs=P("seq", "mic", None, None),
        check_vma=False,
    )
```

time: 347 us -> 330 us (0.951)
  waiting for transfers between devices: 201 us -> 137 us
  blocking collectives: 35.1 us -> 96.9 us
  local copies, waits for them, and re-layouts: 36.6 us -> 26 us
  Pallas kernels: 0 us -> 7.2 us
  matrix products: 42.3 us -> 35.1 us
  starting transfers between devices: 16 us -> 11.1 us
    all_to_all x0 -> x2, blocking collectives: none -> 56.9 us  [the longest x1 41.2 us: body(): lax.all_to_all(projected, 'mic', split_axis=2, concat_axis=0, tiled=True)]
    all_gather x2, waiting for transfers between devices: 97.1 us -> 45 us  [the longest x1 37.6 us: body(): arrived_rows = lax.all_gather(landed[None], 'mic', axis=0, tiled=True)]
    all_to_all x1 -> x0, waiting for transfers between devices: 35.4 us -> none  [body(): lax.all_to_all(projected, 'mic', split_axis=1, concat_axis=0, tiled=True)]
    reduce_scatter x1 -> x2, waiting for transfers between devices: 41.3 us -> 64.7 us  [the longest x1 41.3 us: body(): summed = lax.psum_scatter(result, 'mic', scatter_dimension=0, tiled=True)]
    convert_element_type x3 -> x0, local copies, waits for them, and re-layouts: 13.3 us -> none  [the longest x2 10.1 us: body(): summed = lax.psum_scatter(result.reshape(lax.axis_size('mic') * (seq_coun...]
    pallas_call x0 -> x1, Pallas kernels: none -> 7.2 us  [attend(): pl.pallas_call(attend_kernel, out_shape=jax.ShapeDtypeStruct((mics, rows...]
    sub x1 -> x0, matrix products: 6.56 us -> none  [body(): weights = jnp.exp(scores - row_max)]
    all_gather x0 -> x1, local copies, waits for them, and re-layouts: none -> 5.62 us  [body(): arrived_rows = lax.all_gather(landed[None], 'mic', axis=0, tiled=True)]
  transfers between devices with their start and end apart: 5 -> 5, of which waited for: 5 -> 5; matrix products, arithmetic and copies ran while one was open for 11% -> 4% of each run, Pallas kernels for 0% -> 2%
where the time goes in v1:
time: 330 us; the launch traced here: 329 us
  waiting for transfers between devices  137 us (42%)
  blocking collectives  96.9 us (29%)
  matrix products  35.1 us (11%)
  local copies, waits for them, and re-layouts  26 us (8%)
  between operations  13.2 us (4%)
  starting transfers between devices  11.1 us (3%)
  Pallas kernels  7.2 us (2%)
    reduce_scatter x1, waiting for transfers between devices, body(): summed = lax.psum_scatter(result, 'mic', scatter_dimension=0, tiled=True)  41.3 us
    all_to_all x1, blocking collectives, body(): lax.all_to_all(projected, 'mic', split_axis=2, concat_axis=0, tiled=True)  41.2 us
    all_to_all x1, blocking collectives, body(): lax.all_to_all(buffers, 'seq', split_axis=0, concat_axis=0, tiled=True)  40 us
    all_gather x1, waiting for transfers between devices, body(): arrived_rows = lax.all_gather(landed[None], 'mic', axis=0, tiled=True)  37.6 us
    all_to_all x1, waiting for transfers between devices, body(): lax.all_to_all(summed, 'seq', split_axis=0, concat_axis=0, tiled=True)  26.6 us
    reduce_scatter x1, waiting for transfers between devices, body(): lax.psum_scatter(partial, 'mic', scatter_dimension=0, tiled=True)  23.5 us
    all_to_all x1, blocking collectives, body(): lax.all_to_all(attended_t, 'mic', split_axis=0, concat_axis=2, tiled=True)  15.6 us
    dot_general x1, matrix products, body(): jnp.dot(inner, w_down[0], preferred_element_type=jnp.float32)  11.7 us
  transfers between devices with their start and end apart: 5, of which 5 were waited for; matrix products, arithmetic and copies ran while one was open for 4% of the time, Pallas kernels for 2%

profile of v1, /device:TPU:1, one launch (start us, length us, event | category | flops | bytes accessed | tf_op | source)
XLA Modules:
  0.0 328.8 jit_solution(5238166937692138134)
XLA Ops:
  6.5 0.0 copy-start
  6.5 0.0 all-gather.4.cloned.1.call-start
  6.5 0.7 all-gather.4.cloned.1.call-update
  7.3 0.0 reduce-scatter.3.cloned.1.call-start
  7.3 1.1 copy-done
  8.4 4.7 %convolution_convert_fusion = bf16[2,1536,512]{1,2,0:T(8,128)(2,1)} fusion(bf16[2,512,512]{2,1,0:T(8,128)(2,1)} %param.9, bf16[2,512,1536]{2,1,0:T(8,128)(2,1)S(1)} %copy-done), kind=kOutput, calls=%fused_computation.1 | convolution fusion | flops 1612185600 | bytes 7340032 | tf_op jit(solution)/shard_map/mfc,mce->mef/dot_general | solution.py:71
  13.2 4.6 %copy.17 = bf16[2,1536,4,128]{3,1,0,2:T(8,128)(2,1)} copy(bf16[2,1536,4,128]{1,3,2,0:T(8,128)(2,1)} %bitcast.47) | data formatting | bytes 6291456 | tf_op jit(solution)/shard_map/reshape | solution.py:74
  17.8 41.2 %all_to_all.40 = bf16[2,1536,4,128]{3,1,0,2:T(8,128)(2,1)} all-to-all(bf16[2,1536,4,128]{3,1,0,2:T(8,128)(2,1)} %copy.17), channel_id=1, replica_groups=mesh['mic'=4,'seq'=64] {'mic'}, dimensions={2} | all-to-all | bytes 6291456 | tf_op jit(solution)/shard_map/all_to_all | solution.py:75
  59.0 7.2 %shard_map.91 = bf16[8,512,128]{2,1,0:T(8,128)(2,1)} custom-call(bf16[8,1536,128]{2,1,0:T(8,128)(2,1)} %bitcast.45), custom_call_target="tpu_custom_call" | custom-call | flops 16777216 | bytes 4194304 | tf_op jit(solution)/shard_map/pallas_call | solution.py:48
  66.2 2.3 copy.18
  68.5 15.6 %all_to_all.41 = bf16[4,1024,128]{1,2,0:T(8,128)(2,1)} all-to-all(bf16[4,1024,128]{1,2,0:T(8,128)(2,1)} %copy.18), channel_id=1, replica_groups=mesh['mic'=4,'seq'=64] {'mic'}, dimensions={0} | all-to-all | bytes 2097152 | tf_op jit(solution)/shard_map/all_to_all | solution.py:79
  84.2 7.4 %all-gather.4.cloned.1.call-done = bf16[1024,1024]{1,0:T(8,128)(2,1)} async-done(((bf16[16,1024]{1,0:T(8,128)(2,1)}), bf16[1024,1024]{1,0:T(8,128)(2,1)}) %all-gather.4.cloned.1.call-update) | async-done | bytes 2097168 | tf_op jit(solution)/shard_map/all_gather | solution.py:81
  91.6 0.0 copy-start.2
  91.6 0.0 copy-start.3
  91.6 4.2 %convolution_convert_fusion.2 = bf16[512,1024]{1,0:T(8,128)(2,1)} fusion(bf16[1024,512]{0,1:T(8,128)(2,1)} %bitcast.48, bf16[1024,1024]{1,0:T(8,128)(2,1)} %all-gather.4.cloned.1.call-done), kind=kOutput, calls=%fused_computation.7 | convolution fusion | flops 1074266112 | bytes 4194304 | tf_op jit(solution)/shard_map/dot_general | solution.py:82
  95.8 0.0 reduce-scatter.3.cloned.1.call-update
  95.8 0.0 all-gather.6.cloned.1.call-start
  95.9 0.0 copy-done.2
  95.9 0.1 copy.19
  96.0 0.2 reduce_window_sum.11
  96.2 0.1 copy.21
  96.4 0.1 copy.22
  96.5 23.5 %reduce-scatter.3.cloned.1.call-done = bf16[128,1024]{1,0:T(8,128)(2,1)} async-done(((bf16[512,1024]{1,0:T(8,128)(2,1)}), bf16[128,1024]{1,0:T(8,128)(2,1)}) %reduce-scatter.3.cloned.1.call-update) | async-done | bytes 262160 | tf_op jit(solution)/shard_map/reduce_scatter | solution.py:85
  120.0 1.1 fusion.9
  121.1 0.0 copy-done.3
  121.1 2.3 convolution_convert_fusion.3
  123.4 2.2 reshape.66
  125.6 40.0 %all_to_all.42 = bf16[64,6,1024]{2,1,0:T(8,128)(2,1)S(1)} all-to-all(bf16[64,6,1024]{2,1,0:T(8,128)(2,1)} %reshape.66), channel_id=1, replica_groups=mesh['mic'=4,'seq'=64] {'seq'}, dimensions={0} | all-to-all | bytes 1572864 | tf_op jit(solution)/shard_map/all_to_all | solution.py:109
  165.6 1.3 copy.23
  166.9 0.0 all-gather.6.cloned.1.call-update
  167.0 0.2 reduce-scatter.5.cloned.1.call-start
  167.2 37.6 %all-gather.6.cloned.1.call-done = bf16[256,6,1024]{2,0,1:T(8,128)(2,1)} async-done(((bf16[64,6,1024]{2,0,1:T(8,128)(2,1)}), bf16[256,6,1024]{2,0,1:T(8,128)(2,1)}) %all-gather.6.cloned.1.call-update) | async-done | bytes 3145744 | tf_op jit(solution)/shard_map/all_gather | solution.py:110
  204.8 5.6 %copy.24 = bf16[256,6,1024]{2,1,0:T(8,128)(2,1)} copy(bf16[256,6,1024]{2,0,1:T(8,128)(2,1)} %all-gather.6.cloned.1.call-done) | data formatting | bytes 6291456 | tf_op jit(solution)/shard_map/all_gather | solution.py:110
  210.4 6.3 %reshape.67 = bf16[1536,1024]{1,0:T(8,128)(2,1)} reshape(bf16[256,6,1024]{2,1,0:T(8,128)(2,1)} %copy.24) | data formatting | bytes 6291456 | tf_op jit(solution)/shard_map/reshape | solution.py:111
  216.7 8.6 %fusion.3 = f32[1536,1024]{1,0:T(8,128)} fusion(bf16[1536,1024]{1,0:T(8,128)(2,1)} %reshape.67, bf16[1,1024,1024]{2,1,0:T(8,128)(2,1)} %param.14), kind=kOutput, calls=%fused_computation.5 | convolution fusion | flops 3221225472 | bytes 11534336 | tf_op jit(solution)/shard_map/dot_general | solution.py:112
  225.4 11.7 %convolution_convert_fusion.1 = bf16[1536,1024]{1,0:T(8,128)(2,1)} fusion(f32[1536,1024]{1,0:T(8,128)} %fusion.3, bf16[1536,1024]{1,0:T(8,128)(2,1)} %reshape.67, bf16[1,1024,1024]{2,1,0:T(8,128)(2,1)} %param.16, bf16[1,1024,1024]{2,1,0:T(8,128)(2,1)} %param.15), kind=kOutput, calls=%fused_computation.2 | convolution fusion | flops 6453460992 | bytes 16777216 | tf_op jit(solution)/shard_map/dot_general | solution.py:115
  237.0 0.0 copy-start.1
  237.0 0.0 reduce-scatter.5.cloned.1.call-update
  237.0 41.3 %reduce-scatter.5.cloned.1.call-done = bf16[384,1024]{1,0:T(8,128)(2,1)} async-done(((bf16[1536,1024]{1,0:T(8,128)(2,1)}), bf16[384,1024]{1,0:T(8,128)(2,1)}) %reduce-scatter.5.cloned.1.call-update) | async-done | bytes 786448 | tf_op jit(solution)/shard_map/reduce_scatter | solution.py:116
  278.3 2.2 reshape.68
  280.5 10.8 %all-to-all-start.3 = ((bf16[64,6,1024]{2,1,0:T(8,128)(2,1)}), bf16[64,6,1024]{2,1,0:T(8,128)(2,1)}, u32[]{:S(2)}, u32[]{:S(2)}) async-start(bf16[64,6,1024]{2,1,0:T(8,128)(2,1)} %reshape.68), calls=%async_computation.5 | async-start | bytes 2097152 | tf_op jit(solution)/shard_map/all_to_all | solution.py:118
  291.3 0.0 copy-done.1
  291.3 1.2 fusion.19
  292.6 26.6 %all-to-all-done.3 = bf16[64,6,1024]{2,1,0:T(8,128)(2,1)} async-done(((bf16[64,6,1024]{2,1,0:T(8,128)(2,1)}), bf16[64,6,1024]{2,1,0:T(8,128)(2,1)}, u32[]{:S(2)}, u32[]{:S(2)}) %all-to-all-start.3) | async-done | bytes 786464 | tf_op jit(solution)/shard_map/all_to_all | solution.py:118
  319.2 2.3 fusion.6
  321.5 0.8 fusion.14
  (11 shorter events, 0.2 us)
Async XLA Ops:
  6.5 1.9 copy-start
  6.5 85.0 %all-gather.4.cloned.1.call-start = ((), (), s32[]{:S(2)}) async-start(), calls=%async_computation.6 | async-start | bytes 2129920 | tf_op jit(solution)/shard_map/all_gather | solution.py:81
  7.3 112.7 %reduce-scatter.3.cloned.1.call-start = ((), (), s32[]{:S(2)}) async-start(), calls=%async_computation.7 | async-start | bytes 1310720 | tf_op jit(solution)/shard_map/reduce_scatter | solution.py:85
  91.6 4.3 %copy-start.2 = (s32[1,1,128,2]{2,3,1,0:T(2,128)S(1)}, s32[1,1,128,2]{2,3,1,0:T(2,128)}, u32[]{:S(2)}) copy-start(s32[1,1,128,2]{2,3,1,0:T(2,128)} %param.17) | copy-start | bytes 3076
  91.6 29.5 %copy-start.3 = (f32[1024]{0:T(1024)S(1)}, f32[1024]{0:T(1024)}, u32[]{:S(2)}) copy-start(f32[1024]{0:T(1024)} %param.12) | copy-start | bytes 12292
  95.8 108.9 %all-gather.6.cloned.1.call-start = ((), (), s32[]{:S(2)}) async-start(), calls=%async_computation.9 | async-start | bytes 3932160 | tf_op jit(solution)/shard_map/all_gather | solution.py:110
  167.0 111.3 %reduce-scatter.5.cloned.1.call-start = ((), (), s32[]{:S(2)}) async-start(), calls=%async_computation.8 | async-start | bytes 3932160 | tf_op jit(solution)/shard_map/reduce_scatter | solution.py:116
  237.0 54.3 %copy-start.1 = (bf16[128,1024]{1,0:T(8,128)(2,1)S(1)}, bf16[128,1024]{1,0:T(8,128)(2,1)}, u32[]{:S(2)}) copy-start(bf16[128,1024]{1,0:T(8,128)(2,1)} %reduce-scatter.3.cloned.1.call-done) | copy-start | bytes 786436
  280.5 38.7 %all-to-all-start.3 = ((bf16[64,6,1024]{2,1,0:T(8,128)(2,1)}), bf16[64,6,1024]{2,1,0:T(8,128)(2,1)}, u32[]{:S(2)}, u32[]{:S(2)}) async-start(bf16[64,6,1024]{2,1,0:T(8,128)(2,1)} %reshape.68), calls=%async_computation.5 | async-start | bytes 2097152 | tf_op jit(solution)/shard_map/all_to_all | solution.py:118
Sparse Core Ops, SparseCore 0:
  10.1 81.4 all-gather.3
  96.0 23.9 reduce-scatter.2
  167.1 37.6 all-gather.5
  237.2 41.0 reduce-scatter.4
